TPU v7x, 512 devices: a whole 4x8x8 slice. The times are simulated.
512 devices in a mesh: dp: 32 (over x, z_lo, core), seq: 16 (over z_hi, y).
Axes of the slice: x: 4, y: 8, z: 8 (z_hi: 2, z_lo: 4; z = z_hi * 4 + z_lo), core: 2. Of those that a mesh axis runs over, the one named last changes fastest.
Arguments:
- q_space: bfloat16 [32, 2560, 1152], P('dp', 'seq'), may hold values from -64 to 64
- k_space: bfloat16 [32, 2560, 1152], P('dp', 'seq'), may hold values from -6 to 6
- v_space: bfloat16 [32, 2560, 1152], P('dp', 'seq'), may hold values from -6 to 6
- q_time: bfloat16 [32, 2560, 1152], P('dp', 'seq'), may hold values from -64 to 64
- k_time: bfloat16 [32, 2560, 1152], P('dp', 'seq'), may hold values from -6 to 6
- v_time: bfloat16 [32, 2560, 1152], P('dp', 'seq'), may hold values from -6 to 6
- weight: bfloat16 [1152, 1152], P('dp'), may hold values from -0.1875 to 0.1875
- target: bfloat16 [32, 2560, 1152], P('dp', 'seq'), may hold values from -6 to 6
Outputs:
- grad_q_space: bfloat16 [32, 2560, 1152], P('dp', 'seq')
- grad_k_space: bfloat16 [32, 2560, 1152], P('dp', 'seq')
- grad_v_space: bfloat16 [32, 2560, 1152], P('dp', 'seq')
- grad_q_time: bfloat16 [32, 2560, 1152], P('dp', 'seq')
- grad_k_time: bfloat16 [32, 2560, 1152], P('dp', 'seq')
- grad_v_time: bfloat16 [32, 2560, 1152], P('dp', 'seq')
- weight_grad: float32 [1152, 1152], P('seq')
All inputs are finite; a program needn't handle non-finite values.
Results may differ from a plain program's by a relative error of at most 0.025.
Values may be sent and summed in bfloat16 or wider, within the bound.
A program may use at most 64 MiB of HBM per device.

v0:
```python
import math

import jax
import jax.numpy as jnp
from jax import lax
from jax.sharding import PartitionSpec as P

HEAD_DIM = 72


def form_pair(layout):
    if layout == "space":
        return ("blhe", "bmhe")
    return ("lbhe", "mbhe")


def split_heads(array):
    return array.reshape(array.shape[:-1] + (array.shape[-1] // HEAD_DIM, HEAD_DIM))


def attend_forward(query, key_data, values, layout):
    query_form, key_form = form_pair(layout)
    scaling = 1.0 / math.sqrt(HEAD_DIM)
    logits = (
        jnp.einsum(
            query_form + "," + key_form + "->bhlm",
            query,
            key_data,
            preferred_element_type=jnp.float32,
        )
        * scaling
    )
    row_max = jnp.max(logits, axis=-1, keepdims=True)
    lifted = jnp.exp(logits - row_max)
    attention = lifted / jnp.sum(lifted, axis=-1, keepdims=True)
    rounded = attention.astype(jnp.bfloat16)
    result = jnp.einsum(
        "bhlm," + key_form + "->" + query_form, rounded, values, preferred_element_type=jnp.float32
    )
    return (attention, rounded, result)


def attend_backward(query, key_data, values, attention, rounded, step_grad, layout):
    query_form, key_form = form_pair(layout)
    scaling = 1.0 / math.sqrt(HEAD_DIM)
    upstream = jnp.einsum(
        query_form + "," + key_form + "->bhlm",
        step_grad,
        values,
        preferred_element_type=jnp.float32,
    )
    grad_values = jnp.einsum(
        "bhlm," + query_form + "->" + key_form,
        rounded,
        step_grad,
        preferred_element_type=jnp.float32,
    ).astype(jnp.bfloat16)
    grad_scores = (
        attention * (upstream - jnp.sum(attention * upstream, axis=-1, keepdims=True))
    ).astype(jnp.bfloat16)
    grad_query = (
        jnp.einsum(
            "bhlm," + key_form + "->" + query_form,
            grad_scores,
            key_data,
            preferred_element_type=jnp.float32,
        )
        * scaling
    ).astype(jnp.bfloat16)
    grad_keys = (
        jnp.einsum(
            "bhlm," + query_form + "->" + key_form,
            grad_scores,
            query,
            preferred_element_type=jnp.float32,
        )
        * scaling
    ).astype(jnp.bfloat16)
    return (grad_query, grad_keys, grad_values)


def time_side(time_q, time_k, time_v, out_space, target_rows, full_weight):
    heads_q = split_heads(time_q)
    heads_k = split_heads(time_k)
    heads_v = split_heads(time_v)
    attention_t, rounded_t, result_t = attend_forward(heads_q, heads_k, heads_v, "time")
    combined = (out_space.astype(jnp.float32) + result_t.reshape(out_space.shape)).astype(
        jnp.bfloat16
    )
    projected = jnp.einsum("fnd,dc->fnc", combined, full_weight, preferred_element_type=jnp.float32)
    output_grad = (projected - target_rows.astype(jnp.float32)).astype(jnp.bfloat16)
    step_grad = jnp.einsum(
        "fnc,dc->fnd", output_grad, full_weight, preferred_element_type=jnp.float32
    ).astype(jnp.bfloat16)
    grads_time = attend_backward(
        heads_q, heads_k, heads_v, attention_t, rounded_t, split_heads(step_grad), "time"
    )
    grad_q, grad_k, grad_v = [item.reshape(out_space.shape) for item in grads_time]
    return (step_grad, grad_q, grad_k, grad_v, combined, output_grad)


def shards(q_space, k_space, v_space, q_time, k_time, v_time, weight, target):
    space_q = split_heads(q_space)
    space_k = split_heads(k_space)
    space_v = split_heads(v_space)
    attention_s, rounded_s, result_s = attend_forward(space_q, space_k, space_v, "space")
    out_space = result_s.astype(jnp.bfloat16).reshape(q_space.shape)
    full_weight = lax.all_gather(weight, "dp", axis=0, tiled=True)
    groups = lax.axis_size("seq")
    width = q_space.shape[2]
    per_block = q_space.shape[1] // groups

    def blocked(array):
        return array.reshape(1, groups, per_block, width)

    def per_patch(pieces):
        flat = [item[:, 0] for item in pieces]
        outcome = time_side(flat[0], flat[1], flat[2], flat[3], flat[4], full_weight)
        return tuple((item[:, None] for item in outcome))

    mapped = per_patch(
        (
            lax.all_to_all(blocked(q_time), "seq", split_axis=1, concat_axis=0, tiled=True),
            lax.all_to_all(blocked(k_time), "seq", split_axis=1, concat_axis=0, tiled=True),
            lax.all_to_all(blocked(v_time), "seq", split_axis=1, concat_axis=0, tiled=True),
            lax.all_to_all(blocked(out_space), "seq", split_axis=1, concat_axis=0, tiled=True),
            lax.all_to_all(blocked(target), "seq", split_axis=1, concat_axis=0, tiled=True),
        )
    )
    returned = tuple((item[:, 0] for item in mapped))
    step_grad, grad_qt, grad_kt, grad_vt, combined, output_grad = returned
    home = (
        lax.all_to_all(step_grad, "seq", split_axis=0, concat_axis=1, tiled=True),
        lax.all_to_all(grad_qt, "seq", split_axis=0, concat_axis=1, tiled=True),
        lax.all_to_all(grad_kt, "seq", split_axis=0, concat_axis=1, tiled=True),
        lax.all_to_all(grad_vt, "seq", split_axis=0, concat_axis=1, tiled=True),
    )
    grads_space = attend_backward(
        space_q, space_k, space_v, attention_s, rounded_s, split_heads(home[0]), "space"
    )
    grad_qs, grad_ks, grad_vs = [item.reshape(q_space.shape) for item in grads_space]
    flat_comb = combined.reshape(-1, combined.shape[-1])
    flat_grad = output_grad.reshape(-1, output_grad.shape[-1])
    share = lax.psum_scatter(
        lax.dot_general(
            flat_comb, flat_grad, (((0,), (0,)), ((), ())), preferred_element_type=jnp.float32
        ).astype(jnp.bfloat16),
        "seq",
        scatter_dimension=0,
        tiled=True,
    )
    total = lax.psum(share, "dp").astype(jnp.float32)
    scaling = 1.0 / math.sqrt(lax.axis_size("dp") * lax.axis_size("seq") * q_space.shape[1])
    return (grad_qs, grad_ks, grad_vs, home[1], home[2], home[3], total * scaling)


def solution(mesh):
    return jax.shard_map(
        shards,
        mesh=mesh,
        in_specs=(
            P("dp", "seq", None),
            P("dp", "seq", None),
            P("dp", "seq", None),
            P("dp", "seq", None),
            P("dp", "seq", None),
            P("dp", "seq", None),
            P("dp", None),
            P("dp", "seq", None),
        ),
        out_specs=(
            P("dp", "seq", None),
            P("dp", "seq", None),
            P("dp", "seq", None),
            P("dp", "seq", None),
            P("dp", "seq", None),
            P("dp", "seq", None),
            P("seq", None),
        ),
        check_vma=False,
    )
```

profile of v0, /device:TPU:1, one launch (start us, length us, event | category | flops | bytes accessed | tf_op | source)
XLA Modules:
  0.0 651.3 jit_solution(3526886626338543197)
XLA Ops:
  7.9 1.9 reshape.158
  9.9 16.2 %all-to-all-start.1 = ((bf16[1,16,10,1152]{3,2,0,1:T(8,128)(2,1)}), bf16[1,16,10,1152]{3,2,0,1:T(8,128)(2,1)S(1)}, u32[]{:S(2)}, u32[]{:S(2)}) async-start(bf16[1,16,10,1152]{3,2,0,1:T(8,128)(2,1)} %bitcast.5), calls=%async_computation.1 | async-start | bytes 1179648 | tf_op jit(solution)/shard_map/all_to_all | solution.py:123
  27.0 18.7 %all-to-all-done.1 = bf16[1,16,10,1152]{3,2,0,1:T(8,128)(2,1)S(1)} async-done(((bf16[1,16,10,1152]{3,2,0,1:T(8,128)(2,1)}), bf16[1,16,10,1152]{3,2,0,1:T(8,128)(2,1)S(1)}, u32[]{:S(2)}, u32[]{:S(2)}) %all-to-all-start.1) | async-done | bytes 368672 | tf_op jit(solution)/shard_map/all_to_all | solution.py:123
  45.8 6.1 all-to-all-start.2
  52.1 1.1 copy.132
  53.2 1.1 copy.133
  55.3 15.4 %all-to-all-done.2 = bf16[1,16,10,1152]{3,2,0,1:T(8,128)(2,1)S(1)} async-done(((bf16[1,16,10,1152]{3,2,0,1:T(8,128)(2,1)}), bf16[1,16,10,1152]{3,2,0,1:T(8,128)(2,1)S(1)}, u32[]{:S(2)}, u32[]{:S(2)}) %all-to-all-start.2) | async-done | bytes 368672 | tf_op jit(solution)/shard_map/all_to_all | solution.py:124
  70.7 6.1 all-to-all-start.3
  76.8 2.2 fusion.50
  79.0 2.7 fusion.17
  81.7 1.6 copy.78
  83.3 1.7 reshape_reshape.3
  85.1 9.3 %all-to-all-done.3 = bf16[1,16,10,1152]{3,2,0,1:T(8,128)(2,1)} async-done(((bf16[1,16,10,1152]{3,2,0,1:T(8,128)(2,1)}), bf16[1,16,10,1152]{3,2,0,1:T(8,128)(2,1)}, u32[]{:S(2)}, u32[]{:S(2)}) %all-to-all-start.3) | async-done | bytes 368672 | tf_op jit(solution)/shard_map/all_to_all | solution.py:125
  94.4 6.6 %all-to-all-start = ((bf16[1,16,10,1152]{3,2,0,1:T(8,128)(2,1)}), bf16[1,16,10,1152]{3,2,0,1:T(8,128)(2,1)S(1)}, u32[]{:S(2)}, u32[]{:S(2)}) async-start(bf16[1,16,10,1152]{3,2,0,1:T(8,128)(2,1)} %bitcast.3), calls=%async_computation | async-start | bytes 1179648 | tf_op jit(solution)/shard_map/all_to_all | solution.py:126
  102.0 1.2 reshape.179
  103.2 1.2 reshape.180
  104.5 2.6 reshape.181
  107.1 2.0 fusion.45
  109.1 9.4 %all-to-all-done = bf16[1,16,10,1152]{3,2,0,1:T(8,128)(2,1)S(1)} async-done(((bf16[1,16,10,1152]{3,2,0,1:T(8,128)(2,1)}), bf16[1,16,10,1152]{3,2,0,1:T(8,128)(2,1)S(1)}, u32[]{:S(2)}, u32[]{:S(2)}) %all-to-all-start) | async-done | bytes 368672 | tf_op jit(solution)/shard_map/all_to_all | solution.py:126
  118.5 5.9 all-to-all-start.4
  124.7 1.8 convolution_bitcast_fusion.1
  128.3 3.6 reshape.172
  131.9 8.8 %all-to-all-done.4 = bf16[1,16,10,1152]{3,2,0,1:T(8,128)(2,1)S(1)} async-done(((bf16[1,16,10,1152]{3,2,0,1:T(8,128)(2,1)}), bf16[1,16,10,1152]{3,2,0,1:T(8,128)(2,1)S(1)}, u32[]{:S(2)}, u32[]{:S(2)}) %all-to-all-start.4) | async-done | bytes 368672 | tf_op jit(solution)/shard_map/all_to_all | solution.py:127
  140.8 1.8 fusion.3
  143.3 2.5 fusion.2
  148.7 6.8 %all-to-all-start.5 = ((bf16[16,10,1152]{2,1,0:T(8,128)(2,1)}), bf16[16,10,1152]{2,1,0:T(8,128)(2,1)S(1)}, u32[]{:S(2)}, u32[]{:S(2)}) async-start(bf16[16,10,1152]{2,1,0:T(8,128)(2,1)} %copy.94), calls=%async_computation.5 | async-start | bytes 1179648 | tf_op jit(solution)/shard_map/all_to_all | solution.py:133
  155.5 1.1 reshape.167
  158.0 1.7 reshape.177
  159.8 2.8 multiply_reduce_fusion.2
  162.6 9.7 %all-to-all-done.5 = bf16[16,10,1152]{2,1,0:T(8,128)(2,1)S(1)} async-done(((bf16[16,10,1152]{2,1,0:T(8,128)(2,1)}), bf16[16,10,1152]{2,1,0:T(8,128)(2,1)S(1)}, u32[]{:S(2)}, u32[]{:S(2)}) %all-to-all-start.5) | async-done | bytes 368672 | tf_op jit(solution)/shard_map/all_to_all | solution.py:133
  172.2 7.1 %all-to-all-start.8 = ((bf16[16,10,1152]{2,1,0:T(8,128)(2,1)}), bf16[16,10,1152]{2,1,0:T(8,128)(2,1)}, u32[]{:S(2)}, u32[]{:S(2)}) async-start(bf16[16,10,1152]{2,1,0:T(8,128)(2,1)} %reshape.177), calls=%async_computation.8 | async-start | bytes 1179648 | tf_op jit(solution)/shard_map/all_to_all | solution.py:136
  179.3 1.7 multiply_convert_fusion.1
  181.7 1.8 reshape.175
  184.2 1.7 reshape.176
  185.9 2.5 reshape.163
  188.4 1.4 copy.95
  189.8 9.1 %all-to-all-done.8 = bf16[16,10,1152]{2,1,0:T(8,128)(2,1)} async-done(((bf16[16,10,1152]{2,1,0:T(8,128)(2,1)}), bf16[16,10,1152]{2,1,0:T(8,128)(2,1)}, u32[]{:S(2)}, u32[]{:S(2)}) %all-to-all-start.8) | async-done | bytes 368672 | tf_op jit(solution)/shard_map/all_to_all | solution.py:136
  199.0 7.3 %all-to-all-start.7 = ((bf16[16,10,1152]{2,1,0:T(8,128)(2,1)}), bf16[16,10,1152]{2,1,0:T(8,128)(2,1)S(1)}, u32[]{:S(2)}, u32[]{:S(2)}) async-start(bf16[16,10,1152]{2,1,0:T(8,128)(2,1)} %reshape.176), calls=%async_computation.7 | async-start | bytes 1179648 | tf_op jit(solution)/shard_map/all_to_all | solution.py:135
  206.3 2.0 multiply_reduce_fusion
  208.9 17.0 %all-to-all-done.7 = bf16[16,10,1152]{2,1,0:T(8,128)(2,1)S(1)} async-done(((bf16[16,10,1152]{2,1,0:T(8,128)(2,1)}), bf16[16,10,1152]{2,1,0:T(8,128)(2,1)S(1)}, u32[]{:S(2)}, u32[]{:S(2)}) %all-to-all-start.7) | async-done | bytes 368672 | tf_op jit(solution)/shard_map/all_to_all | solution.py:135
  226.0 6.7 %all-to-all-start.6 = ((bf16[16,10,1152]{2,1,0:T(8,128)(2,1)}), bf16[16,10,1152]{2,1,0:T(8,128)(2,1)}, u32[]{:S(2)}, u32[]{:S(2)}) async-start(bf16[16,10,1152]{2,1,0:T(8,128)(2,1)} %reshape.175), calls=%async_computation.6 | async-start | bytes 1179648 | tf_op jit(solution)/shard_map/all_to_all | solution.py:134
  232.7 3.2 convolution_convert_fusion.2
  235.9 2.0 copy.119
  239.3 138.4 %reduce-scatter.4.cloned.1.call-done = bf16[72,1152]{1,0:T(8,128)(2,1)} async-done(((bf16[1152,1152]{1,0:T(8,128)(2,1)}), bf16[72,1152]{1,0:T(8,128)(2,1)}) %reduce-scatter.4.cloned.1.call-update) | async-done | bytes 165904
  379.2 1.9 all_to_all.35
  382.0 1.9 all_to_all.31
  384.0 259.1 %all-reduce.3.cloned.1.call-done = bf16[72,1152]{1,0:T(8,128)(2,1)} async-done(((bf16[72,1152]{1,0:T(8,128)(2,1)}), bf16[72,1152]{1,0:T(8,128)(2,1)}) %all-reduce.3.cloned.1.call-update) | async-done | bytes 165904 | tf_op jit(solution)/shard_map/psum | solution.py:152
  643.1 1.7 convert_multiply_fusion
  (91 shorter events, 16.7 us)
Async XLA Ops:
  7.2 18.9 %copy-start.25 = (bf16[1,160,1152]{2,1,0:T(8,128)(2,1)S(1)}, bf16[1,160,1152]{2,1,0:T(8,128)(2,1)}, u32[]{:S(2)}) copy-start(bf16[1,160,1152]{2,1,0:T(8,128)(2,1)} %param.12) | copy-start | bytes 1105924
  7.2 121.2 %all-gather.3.cloned.1.call-start = ((), (), s32[]{:S(2)}) async-start(), calls=%async_computation.11 | async-start | bytes 3041280 | tf_op jit(solution)/shard_map/all_gather | solution.py:108
  9.9 35.9 %all-to-all-start.1 = ((bf16[1,16,10,1152]{3,2,0,1:T(8,128)(2,1)}), bf16[1,16,10,1152]{3,2,0,1:T(8,128)(2,1)S(1)}, u32[]{:S(2)}, u32[]{:S(2)}) async-start(bf16[1,16,10,1152]{3,2,0,1:T(8,128)(2,1)} %bitcast.5), calls=%async_computation.1 | async-start | bytes 1179648 | tf_op jit(solution)/shard_map/all_to_all | solution.py:123
  26.1 25.8 %copy-start.26 = (bf16[1,160,1152]{2,1,0:T(8,128)(2,1)S(1)}, bf16[1,160,1152]{2,1,0:T(8,128)(2,1)}, u32[]{:S(2)}) copy-start(bf16[1,160,1152]{2,1,0:T(8,128)(2,1)} %param.8) | copy-start | bytes 1105924
  26.1 26.0 %copy-start.27 = (bf16[1,160,1152]{2,1,0:T(8,128)(2,1)S(1)}, bf16[1,160,1152]{2,1,0:T(8,128)(2,1)}, u32[]{:S(2)}) copy-start(bf16[1,160,1152]{2,1,0:T(8,128)(2,1)} %param.9) | copy-start | bytes 1105924
  45.7 7.5 %copy-start.12 = (bf16[1,16,10,1152]{3,2,0,1:T(8,128)(2,1)}, bf16[1,16,10,1152]{3,2,0,1:T(8,128)(2,1)S(1)}, u32[]{:S(2)}) copy-start(bf16[1,16,10,1152]{3,2,0,1:T(8,128)(2,1)S(1)} %all-to-all-done.1) | copy-start | bytes 1105924
  45.8 7.5 %copy-start.28 = (bf16[1,160,1152]{2,1,0:T(8,128)(2,1)S(1)}, bf16[1,160,1152]{2,1,0:T(8,128)(2,1)}, u32[]{:S(2)}) copy-start(bf16[1,160,1152]{2,1,0:T(8,128)(2,1)} %param.10) | copy-start | bytes 1105924
  45.8 24.9 %all-to-all-start.2 = ((bf16[1,16,10,1152]{3,2,0,1:T(8,128)(2,1)}), bf16[1,16,10,1152]{3,2,0,1:T(8,128)(2,1)S(1)}, u32[]{:S(2)}, u32[]{:S(2)}) async-start(bf16[1,16,10,1152]{3,2,0,1:T(8,128)(2,1)} %bitcast.6), calls=%async_computation.2 | async-start | bytes 1179648 | tf_op jit(solution)/shard_map/all_to_all | solution.py:124
  52.1 24.7 %copy-start.7 = (bf16[1,160,1152]{1,2,0:T(8,128)(2,1)}, bf16[1,160,1152]{1,2,0:T(8,128)(2,1)S(1)}, u32[]{:S(2)}) copy-start(bf16[1,160,1152]{1,2,0:T(8,128)(2,1)S(1)} %copy.131) | copy-start | bytes 1105924
  52.1 2.2 copy-start.29
  70.7 6.1 copy-start.15
  70.7 23.7 %all-to-all-start.3 = ((bf16[1,16,10,1152]{3,2,0,1:T(8,128)(2,1)}), bf16[1,16,10,1152]{3,2,0,1:T(8,128)(2,1)}, u32[]{:S(2)}, u32[]{:S(2)}) async-start(bf16[1,16,10,1152]{3,2,0,1:T(8,128)(2,1)} %bitcast.7), calls=%async_computation.3 | async-start | bytes 1179648 | tf_op jit(solution)/shard_map/all_to_all | solution.py:125
  79.0 2.7 copy-start
  83.3 17.7 %copy-start.30 = (bf16[1,160,1152]{2,1,0:T(8,128)(2,1)S(1)}, bf16[1,160,1152]{2,1,0:T(8,128)(2,1)}, u32[]{:S(2)}) copy-start(bf16[1,160,1152]{2,1,0:T(8,128)(2,1)} %param.15) | copy-start | bytes 1105924
  85.1 16.9 %copy-start.13 = (bf16[1,16,10,1152]{3,2,0,1:T(8,128)(2,1)S(1)}, bf16[1,16,10,1152]{3,2,0,1:T(8,128)(2,1)}, u32[]{:S(2)}) copy-start(bf16[1,16,10,1152]{3,2,0,1:T(8,128)(2,1)} %copy-done.12) | copy-start | bytes 1105924
  94.4 24.1 %all-to-all-start = ((bf16[1,16,10,1152]{3,2,0,1:T(8,128)(2,1)}), bf16[1,16,10,1152]{3,2,0,1:T(8,128)(2,1)S(1)}, u32[]{:S(2)}, u32[]{:S(2)}) async-start(bf16[1,16,10,1152]{3,2,0,1:T(8,128)(2,1)} %bitcast.3), calls=%async_computation | async-start | bytes 1179648 | tf_op jit(solution)/shard_map/all_to_all | solution.py:126
  101.1 2.2 copy-start.16
  103.2 5.9 copy-start.3
  104.5 4.6 copy-start.5
  107.1 17.6 %copy-start.18 = (bf16[16,10,16,72]{3,2,1,0:T(8,128)(2,1)}, bf16[16,10,16,72]{3,2,1,0:T(8,128)(2,1)S(1)}, u32[]{:S(2)}) copy-start(bf16[16,10,16,72]{3,2,1,0:T(8,128)(2,1)S(1)} %reshape.181) | copy-start | bytes 1105924
  118.5 22.2 %all-to-all-start.4 = ((bf16[1,16,10,1152]{3,2,0,1:T(8,128)(2,1)}), bf16[1,16,10,1152]{3,2,0,1:T(8,128)(2,1)S(1)}, u32[]{:S(2)}, u32[]{:S(2)}) async-start(bf16[1,16,10,1152]{3,2,0,1:T(8,128)(2,1)} %bitcast.10), calls=%async_computation.4 | async-start | bytes 1179648 | tf_op jit(solution)/shard_map/all_to_all | solution.py:127
  124.5 253.2 %reduce-scatter.4.cloned.1.call-start = ((), (), s32[]{:S(2)}) async-start(), calls=%async_computation.12 | async-start | bytes 2820096
  140.8 2.5 copy-start.24
  142.5 0.7 copy-start.22
  145.8 1.0 copy-start.23
  148.7 8.8 %copy-start.17 = (f32[10,16,16,16]{2,3,1,0:T(8,128)S(1)}, f32[10,16,16,16]{2,3,1,0:T(8,128)}, u32[]{:S(2)}) copy-start(f32[10,16,16,16]{2,3,1,0:T(8,128)} %get-tuple-element.29) | copy-start | bytes 491524
  148.7 23.5 %all-to-all-start.5 = ((bf16[16,10,1152]{2,1,0:T(8,128)(2,1)}), bf16[16,10,1152]{2,1,0:T(8,128)(2,1)S(1)}, u32[]{:S(2)}, u32[]{:S(2)}) async-start(bf16[16,10,1152]{2,1,0:T(8,128)(2,1)} %copy.94), calls=%async_computation.5 | async-start | bytes 1179648 | tf_op jit(solution)/shard_map/all_to_all | solution.py:133
  156.7 0.8 copy-start.20
  157.8 1.9 copy-start.19
  172.2 8.8 %copy-start.14 = (bf16[16,10,1152]{2,1,0:T(8,128)(2,1)}, bf16[16,10,1152]{2,1,0:T(8,128)(2,1)S(1)}, u32[]{:S(2)}) copy-start(bf16[16,10,1152]{2,1,0:T(8,128)(2,1)S(1)} %all-to-all-done.5) | copy-start | bytes 1105924
  172.2 26.7 %all-to-all-start.8 = ((bf16[16,10,1152]{2,1,0:T(8,128)(2,1)}), bf16[16,10,1152]{2,1,0:T(8,128)(2,1)}, u32[]{:S(2)}, u32[]{:S(2)}) async-start(bf16[16,10,1152]{2,1,0:T(8,128)(2,1)} %reshape.177), calls=%async_computation.8 | async-start | bytes 1179648 | tf_op jit(solution)/shard_map/all_to_all | solution.py:136
  179.3 1.7 copy-start.6
  181.5 2.0 copy-start.4
  185.9 20.4 %copy-start.1 = (f32[16,160,160]{1,2,0:T(8,128)S(1)}, f32[16,160,160]{1,2,0:T(8,128)}, u32[]{:S(2)}) copy-start(f32[16,160,160]{1,2,0:T(8,128)} %copy-done) | copy-start | bytes 4915204
  199.0 27.0 %all-to-all-start.7 = ((bf16[16,10,1152]{2,1,0:T(8,128)(2,1)}), bf16[16,10,1152]{2,1,0:T(8,128)(2,1)S(1)}, u32[]{:S(2)}, u32[]{:S(2)}) async-start(bf16[16,10,1152]{2,1,0:T(8,128)(2,1)} %reshape.176), calls=%async_computation.7 | async-start | bytes 1179648 | tf_op jit(solution)/shard_map/all_to_all | solution.py:135
  206.3 2.1 copy-start.2
  208.4 24.3 %copy-start.21 = (bf16[160,16,72]{0,2,1:T(8,128)(2,1)S(1)}, bf16[160,16,72]{0,2,1:T(8,128)(2,1)}, u32[]{:S(2)}) copy-start(bf16[160,16,72]{0,2,1:T(8,128)(2,1)} %copy.95) | copy-start | bytes 1105924
  226.0 10.0 %copy-start.10 = (bf16[16,10,1152]{2,1,0:T(8,128)(2,1)}, bf16[16,10,1152]{2,1,0:T(8,128)(2,1)S(1)}, u32[]{:S(2)}) copy-start(bf16[16,10,1152]{2,1,0:T(8,128)(2,1)S(1)} %all-to-all-done.7) | copy-start | bytes 1105924
  226.0 156.1 %all-to-all-start.6 = ((bf16[16,10,1152]{2,1,0:T(8,128)(2,1)}), bf16[16,10,1152]{2,1,0:T(8,128)(2,1)}, u32[]{:S(2)}, u32[]{:S(2)}) async-start(bf16[16,10,1152]{2,1,0:T(8,128)(2,1)} %reshape.175), calls=%async_computation.6 | async-start | bytes 1179648 | tf_op jit(solution)/shard_map/all_to_all | solution.py:134
  232.7 5.3 copy-start.9
  232.7 410.4 %all-reduce.3.cloned.1.call-start = ((), (), s32[]{:S(2)}) async-start(), calls=%async_computation.10 | async-start | bytes 331776 | tf_op jit(solution)/shard_map/psum | solution.py:152
  238.0 139.8 %copy-start.8 = (bf16[1,160,1152]{1,2,0:T(8,128)(2,1)S(1)}, bf16[1,160,1152]{1,2,0:T(8,128)(2,1)}, u32[]{:S(2)}) copy-start(bf16[1,160,1152]{1,2,0:T(8,128)(2,1)} %copy-done.7) | copy-start | bytes 1105924
  378.3 2.9 copy-start.11
Sparse Core Ops, SparseCore 0:
  10.2 93.8 all-gather.2
  145.9 231.7 reduce-scatter.3
  380.9 262.1 all-reduce.2
where the time goes:
time: 654 us; the launch traced here: 651 us
  waiting for transfers between devices  496 us (76%)
  starting transfers between devices  69.2 us (11%)
  local copies, waits for them, and re-layouts  43.3 us (7%)
  matrix products  24 us (4%)
  between operations  14.3 us (2%)
    psum x1, waiting for transfers between devices, shards(): total = lax.psum(share, 'dp').astype(jnp.float32)  259 us
    unnamed x4, waiting for transfers between devices  139 us
    all_to_all x1, waiting for transfers between devices, shards(): lax.all_to_all(blocked(q_time), 'seq', split_axis=1, concat_axis=0, tiled...  18.7 us
    all_to_all x1, waiting for transfers between devices, shards(): lax.all_to_all(grad_kt, 'seq', split_axis=0, concat_axis=1, tiled=True)  17 us
    all_to_all x1, starting transfers between devices, shards(): lax.all_to_all(blocked(q_time), 'seq', split_axis=1, concat_axis=0, tiled...  16.2 us
    all_to_all x1, waiting for transfers between devices, shards(): lax.all_to_all(blocked(k_time), 'seq', split_axis=1, concat_axis=0, tiled...  15.4 us
  transfers between devices with their start and end apart: 12, of which 10 were waited for; matrix products, arithmetic and copies ran while one was open for 9% of the time, Pallas kernels for 0%

commit v1 on v0

v1 whole, which is shorter than its diff:
```python
import functools
import math

import jax
import jax.numpy as jnp
from jax import lax
from jax.experimental import pallas as pl
from jax.experimental.pallas import tpu as pltpu
from jax.sharding import PartitionSpec as P

HEADS = 16
HEAD_DIM = 72
D = 1152
TOK = 160
MAIN = 128
SCALING = 1.0 / math.sqrt(HEAD_DIM)
BF = jnp.bfloat16
F32 = jnp.float32
MESH = pl.DeviceIdType.MESH
MQ, MK, MV, MTQ, MA, MTA, MO, MTO, MG, MTG = 0, 1, 2, 3, 4, 5, 6, 7, 8, 17
N_MSG = 18


def dot_nn(a, b):
    return lax.dot_general(a, b, (((1,), (0,)), ((), ())), preferred_element_type=F32)


def dot_nt(a, b):
    return lax.dot_general(a, b, (((1,), (1,)), ((), ())), preferred_element_type=F32)


def dot_tn(a, b):
    return lax.dot_general(a, b, (((0,), (0,)), ((), ())), preferred_element_type=F32)


def window(head):
    start = jnp.minimum((9 * head) // 16, 7) * 128
    lanes = lax.broadcasted_iota(jnp.int32, (1, 256), 1) + start
    inside = jnp.logical_and(lanes >= HEAD_DIM * head, lanes < HEAD_DIM * head + HEAD_DIM)
    return pl.ds(pl.multiple_of(start, 128), 256), inside


def get(ref, cols):
    value = ref[:, :, cols]
    return value.reshape(8 * ref.shape[0], value.shape[2])


def put(ref, cols, value):
    ref[:, :, cols] = value.astype(BF).reshape(ref.shape[0], 8, value.shape[1])


def put_head(ref, cols, inside, value):
    put(ref, cols, jnp.where(inside, value, get(ref, cols).astype(F32)))


def forward_head(head, q_ref, k_ref, v_ref, bias_ref, probs_ref, out_ref):
    cols, inside = window(head)
    chosen = inside.astype(F32).astype(BF)
    logits = dot_nt(get(q_ref, cols) * chosen, get(k_ref, cols)) * SCALING
    if bias_ref is not None:
        logits = logits + bias_ref[...]
    lifted = jnp.exp(logits - jnp.max(logits, axis=-1, keepdims=True))
    probs = lifted * (1.0 / jnp.sum(lifted, axis=-1, keepdims=True))
    probs_ref[head] = probs
    put_head(out_ref, cols, inside, dot_nn(probs.astype(BF), get(v_ref, cols)))


def backward_head(head, q_ref, k_ref, v_ref, probs_ref, step_ref, gq_ref, gk_ref, gv_ref):
    cols, inside = window(head)
    chosen = inside.astype(F32).astype(BF)
    step = get(step_ref, cols)
    probs = probs_ref[head]
    upstream = dot_nt(step * chosen, get(v_ref, cols))
    put_head(gv_ref, cols, inside, dot_tn(probs.astype(BF), step))
    scores = (probs * (upstream - jnp.sum(probs * upstream, axis=-1, keepdims=True))).astype(BF)
    put_head(gq_ref, cols, inside, dot_nn(scores, get(k_ref, cols)) * SCALING)
    put_head(gk_ref, cols, inside, dot_tn(scores, get(q_ref, cols)) * SCALING)


def for_heads(first, last, step):
    def pair(i, carry):
        step(first + 2 * i)
        step(first + 2 * i + 1)
        return carry

    lax.fori_loop(0, (last - first) // 2, pair, 0)


def iota(shape, axis):
    return lax.broadcasted_iota(jnp.int32, shape, axis)


def kernel(
    qs, ks, vs, qt, kt, vt, w_own, target,
    gqs, gks, gvs, gqt, gkt, gvt, wg,
    wb, w, rq, rk, rv, ra, rtq, rta, tq, ta, to, tg, space, over, step_b, step_f,
    ot, ro, rto, comb, gradp, gq, gk, gv, rgq, rgk, rgv, rtg, probs_s, probs_t, bias,
    wgp, r1, half, r2, h2, r3, h3, r4, h4, r5,
    ssem, rsem, wsend, wrecv, csend, crecv, rsend, rrecv,
):
    dp = lax.axis_index("dp")
    s = lax.axis_index("seq")
    core = lax.rem(dp, 2)
    chip = dp // 2
    x = chip // 4
    zl = lax.rem(chip, 4)
    zh = s // 8
    y = lax.rem(s, 8)

    def device(x_, zl_, core_, zh_, y_):
        return ((x_ * 4 + zl_) * 2 + core_, zh_ * 8 + y_)

    def plus(value, k, n):
        return lax.rem(value + k, n)

    sibling = device(x, zl, 1 - core, zh, y)

    barrier = pltpu.get_barrier_semaphore()

    def greet(who):
        pl.semaphore_signal(barrier, inc=1, device_id=who, device_id_type=MESH)

    for k in range(1, 16):
        greet((dp, plus(s, k, 16)))
    for k in range(1, 4):
        greet(device(x, plus(zl, k, 4), core, zh, y))
        greet(device(x, plus(zl, k, 4), core, 1 - zh, y))
        greet(device(plus(x, k, 4), zl, core, zh, y))
        greet(device(plus(x, k, 4), zl, 1 - core, zh, y))
    greet(sibling)
    pl.semaphore_wait(barrier, 28)

    def to_peer(msg, src, dst, peer, cols=None):
        a, b = src.at[peer], dst.at[s]
        if cols is not None:
            a, b = src.at[peer, :, cols], dst.at[s, :, cols]
        return pltpu.make_async_remote_copy(
            src_ref=a, dst_ref=b, send_sem=ssem.at[msg, peer], recv_sem=rsem.at[msg, s],
            device_id=(dp, peer), device_id_type=MESH,
        )

    def from_peer(msg, src, dst, peer, cols=None):
        a, b = src.at[peer], dst.at[peer]
        if cols is not None:
            a, b = src.at[peer, :, cols], dst.at[peer, :, cols]
        return pltpu.make_async_remote_copy(
            src_ref=a, dst_ref=b, send_sem=ssem.at[msg, peer], recv_sem=rsem.at[msg, peer],
            device_id=(dp, peer), device_id_type=MESH,
        )

    def scatter(items):
        def one(k, carry):
            peer = plus(s, k, 16)
            for msg, src, dst, cols in items:
                to_peer(msg, src, dst, peer, cols).start()
            return carry

        lax.fori_loop(1, 16, one, 0)
        for msg, src, dst, cols in items:
            if cols is None:
                dst[s] = src[s]
            else:
                dst[s, :, cols] = src[s, :, cols]

    def gathered(items):
        def one(k, carry):
            peer = plus(s, k, 16)
            for msg, src, dst, cols in items:
                from_peer(msg, src, dst, peer, cols).wait_recv()
            return carry

        lax.fori_loop(1, 16, one, 0)

    def drained(items):
        def one(k, carry):
            peer = plus(s, k, 16)
            for msg, src, dst, cols in items:
                to_peer(msg, src, dst, peer, cols).wait_send()
            return carry

        lax.fori_loop(1, 16, one, 0)

    qkv_items = [(MQ, qt, rq, None), (MK, kt, rk, None), (MV, vt, rv, None)]
    tq_items = [(MTQ, tq, rtq, None)]
    a_items = [(MA, over, ra, None), (MTA, ta, rta, None)]
    o_items = [(MO, ot, ro, None), (MTO, to, rto, None)]
    thirds = [pl.ds(384 * c, 384) for c in range(3)]
    g_items = [
        [
            (MG + 3 * c, gq, rgq, thirds[c]),
            (MG + 3 * c + 1, gk, rgk, thirds[c]),
            (MG + 3 * c + 2, gv, rgv, thirds[c]),
        ]
        for c in range(3)
    ]
    tg_items = [(MTG, tg, rtg, None)]

    def w_copy(src, slot, k, who):
        return pltpu.make_async_remote_copy(
            src_ref=src, dst_ref=wb.at[core, slot], send_sem=wsend.at[k], recv_sem=wrecv.at[slot],
            device_id=who, device_id_type=MESH,
        )

    def w_start():
        for k in range(1, 4):
            w_copy(w_own, chip, k - 1, device(x, plus(zl, k, 4), core, zh, y)).start()
        for k in range(1, 4):
            w_copy(w_own, chip, 2 + k, device(plus(x, k, 4), zl, core, zh, y)).start()
        wb[core, chip] = w_own[...]

    def w_core(group):
        part = wb.at[core, pl.ds(4 * group, 4)]
        return pltpu.make_async_remote_copy(
            src_ref=part, dst_ref=part, send_sem=csend.at[group], recv_sem=crecv.at[group],
            device_id=sibling, device_id_type=MESH,
        )

    def w_other(group):
        part = wb.at[1 - core, pl.ds(4 * group, 4)]
        return pltpu.make_async_remote_copy(
            src_ref=part, dst_ref=part, send_sem=csend.at[group], recv_sem=crecv.at[group],
            device_id=sibling, device_id_type=MESH,
        )

    def w_forward():
        for j in range(1, 4):
            slot = x * 4 + plus(zl, j, 4)
            part = wb.at[core, slot]
            w_copy(part, slot, 0, sibling).wait_recv()
            for k in range(1, 4):
                who = device(plus(x, k, 4), zl, core, zh, y)
                w_copy(part, slot, 3 * j + 2 + k, who).start()
        w_core(x).start()

    def w_share():
        for k in range(1, 4):
            group = plus(x, k, 4)
            for j in range(4):
                slot = group * 4 + j
                w_copy(wb.at[core, slot], slot, 0, sibling).wait_recv()
            w_core(group).start()

    def w_finish():
        for group in range(4):
            w_other(group).wait_recv()

        def lay(i, carry):
            slots = [wb[0, 2 * i], wb[1, 2 * i], wb[0, 2 * i + 1], wb[1, 2 * i + 1]]
            w[pl.ds(pl.multiple_of(144 * i, 16), 144), :] = jnp.concatenate(slots, axis=0)
            return carry

        lax.fori_loop(0, 8, lay, 0)

    def w_drained():
        for k in range(6):
            w_copy(w_own, chip, k, sibling).wait_send()
        for k in range(6, 15):
            w_copy(w_own, chip, k, sibling).wait_send()
        for group in range(4):
            w_core(group).wait_send()

    def packer():
        i, m = iota((128, 96), 0), iota((128, 96), 1)
        r = lax.rem(i, 8)
        source = 32 * (r // 2) + 2 * (i // 8) + lax.rem(r, 2)
        return jnp.where(jnp.logical_and(m == source, r < 6), 1.0, 0.0).astype(BF)

    def unpacker(k):
        i, m = iota((32, 128), 0), iota((32, 128), 1)
        return jnp.where(m == 8 * (i // 2) + 2 * k + lax.rem(i, 2), 1.0, 0.0).astype(BF)

    every = pl.ds(0, D)

    def last_rows(part, cols):
        value = part[16:20, :, cols]
        return value.reshape(32, value.shape[2])

    def whole(ref):
        return ref[...].reshape(128, ref.shape[2])

    def pack(stack, dst):
        dst[...] = dot_nn(packer(), stack).astype(BF).reshape(dst.shape)

    def unpack(src, k, part, cols):
        part[16:20, :, cols] = dot_nn(unpacker(k), whole(src)).astype(BF).reshape(4, 8, src.shape[2])

    def pack_arrays(parts, dst):
        pack(jnp.concatenate([last_rows(p, every) for p in parts], axis=0), dst)

    def unpack_arrays(src, parts):
        for k, part in enumerate(parts):
            unpack(src, k, part, every)

    def pack_thirds(part, dst):
        pack(jnp.concatenate([last_rows(part, thirds[g]) for g in range(3)], axis=0), dst)

    def unpack_thirds(src, part):
        for g in range(3):
            unpack(src, g, part, thirds[g])

    def in_thirds(step):
        def one(c, carry):
            step(pl.ds(pl.multiple_of(384 * c, 128), 384))
            return carry

        lax.fori_loop(0, 3, one, 0)

    w_start()
    scatter(qkv_items)
    pack_arrays([qt, kt, vt], tq)
    scatter(tq_items)

    i, m = iota((TOK, TOK), 0), iota((TOK, TOK), 1)
    patch_i = jnp.where(i < MAIN, lax.rem(i, 8), 8 + lax.rem(i, 2))
    patch_m = jnp.where(m < MAIN, lax.rem(m, 8), 8 + lax.rem(m, 2))
    bias[...] = jnp.where(patch_i == patch_m, 0.0, -1e30)

    def space_forward(h):
        forward_head(h, qs, ks, vs, None, probs_s, space)

    for_heads(0, 6, space_forward)
    w_forward()
    for_heads(6, 16, space_forward)
    w_share()
    w_finish()

    def project_space(cols):
        product = dot_nn(get(space, every), w[:, cols])
        put(gradp, cols, product - get(target, cols).astype(F32))

    in_thirds(project_space)

    def back_space(cols):
        put(over, cols, dot_nt(get(gradp, every), w[cols, :]))

    in_thirds(back_space)
    pack_thirds(over, ta)
    scatter(a_items)

    gathered(qkv_items)
    gathered(tq_items)
    unpack_arrays(rtq, [rq, rk, rv])
    for_heads(0, 16, lambda h: forward_head(h, rq, rk, rv, bias, probs_t, ot))
    pack_thirds(ot, to)
    scatter(o_items)

    def project_time(cols):
        put(gradp, cols, dot_nn(get(ot, every), w[:, cols]))

    in_thirds(project_time)
    gathered(a_items)
    unpack_thirds(rta, ra)

    def back_time(cols):
        share = dot_nt(get(gradp, every), w[cols, :])
        put(step_b, cols, share + get(ra, cols).astype(F32))

    in_thirds(back_time)

    def time_backward(h):
        backward_head(h, rq, rk, rv, probs_t, step_b, gq, gk, gv)

    def send_grads(c):
        scatter(g_items[c])

    for_heads(0, 6, time_backward)
    send_grads(0)

    gathered(o_items)
    unpack_thirds(rto, ro)
    comb[...] = (space[...].astype(F32) + ro[...].astype(F32)).astype(BF)

    def project_all(cols):
        product = dot_nn(get(comb, every), w[:, cols])
        put(gradp, cols, product - get(target, cols).astype(F32))

    in_thirds(project_all)

    def to_sibling(j):
        rows = pl.ds(pl.multiple_of(576 * (1 - core) + 144 * j, 16), 144)
        return pltpu.make_async_remote_copy(
            src_ref=wgp.at[rows], dst_ref=r1.at[pl.ds(144 * j, 144)],
            send_sem=rsend.at[j], recv_sem=rrecv.at[j], device_id=sibling, device_id_type=MESH,
        )

    def x_window(x_):
        return pl.ds(pl.multiple_of(256 * x_, 128), 384)

    def to_x(j, k):
        x_ = plus(x, k, 4)
        rows = pl.ds(144 * j, 144)
        return pltpu.make_async_remote_copy(
            src_ref=half.at[rows, x_window(x_)], dst_ref=r2.at[k - 1, rows],
            send_sem=rsend.at[4 + 3 * j + k - 1], recv_sem=rrecv.at[4 + 3 * j + k - 1],
            device_id=device(x_, zl, core, zh, y), device_id_type=MESH,
        )

    def to_y(k):
        y_ = plus(y, k, 8)
        return pltpu.make_async_remote_copy(
            src_ref=h2.at[y_], dst_ref=r3.at[k - 1],
            send_sem=rsend.at[15 + k], recv_sem=rrecv.at[15 + k],
            device_id=device(x, zl, core, zh, y_), device_id_type=MESH,
        )

    def to_z(k, same):
        zh_ = zh if same else 1 - zh
        slot = k - 1 if same else 3 + k
        return pltpu.make_async_remote_copy(
            src_ref=h3, dst_ref=r4.at[slot], send_sem=rsend.at[23 + slot],
            recv_sem=rrecv.at[23 + slot], device_id=device(x, plus(zl, k, 4), core, zh_, y),
            device_id_type=MESH,
        )

    def to_all(k, flip):
        slot = k - 1 if flip == 0 else 3 + k
        return pltpu.make_async_remote_copy(
            src_ref=h4, dst_ref=r5.at[x], send_sem=rsend.at[31 + slot], recv_sem=rrecv.at[31 + x],
            device_id=device(plus(x, k, 4), zl, core if flip == 0 else 1 - core, zh, y),
            device_id_type=MESH,
        )

    def from_all(x_):
        return pltpu.make_async_remote_copy(
            src_ref=h4, dst_ref=r5.at[x_], send_sem=rsend.at[31], recv_sem=rrecv.at[31 + x_],
            device_id=sibling, device_id_type=MESH,
        )

    def terms(j, carry):
        rows = pl.ds(pl.multiple_of(128 * j, 128), 128)
        wgp[rows, :] = dot_tn(get(comb, rows), get(gradp, every)).astype(BF)
        return carry

    lax.fori_loop(0, 9, terms, 0)
    for j in range(4):
        to_sibling(j).start()

    def back_all(cols):
        put(step_f, cols, dot_nt(get(gradp, every), w[cols, :]))

    in_thirds(back_all)

    for j in range(4):
        to_sibling(j).wait_recv()
        rows = pl.ds(144 * j, 144)
        own = wgp[pl.ds(pl.multiple_of(576 * core + 144 * j, 16), 144), :]
        half[rows, :] = (own.astype(F32) + r1[rows, :].astype(F32)).astype(BF)
        for k in range(1, 4):
            to_x(j, k).start()

    for_heads(6, 12, time_backward)
    send_grads(1)
    for_heads(12, 16, time_backward)
    send_grads(2)
    pack_arrays([gq, gk, gv], tg)
    scatter(tg_items)

    for j in range(4):
        for k in range(1, 4):
            to_x(j, k).wait_recv()
        for i in range(2):
            rows = pl.ds(144 * j + 72 * i, 72)
            total = half[rows, x_window(x)].astype(F32)
            for k in range(1, 4):
                total = total + r2[k - 1, rows, :].astype(F32)
            h2[2 * j + i] = total.astype(BF)
    for k in range(1, 8):
        to_y(k).start()

    def space_backward(h):
        backward_head(h, qs, ks, vs, probs_s, step_f, gqs, gks, gvs)

    for_heads(0, 8, space_backward)

    total = h2[y].astype(F32)
    for k in range(1, 8):
        to_y(k).wait_recv()
        total = total + r3[k - 1].astype(F32)
    h3[...] = total.astype(BF)

    @pl.when(zh == core)
    def _():
        for k in range(1, 4):
            to_z(k, True).start()

    @pl.when(zh != core)
    def _():
        for k in range(4):
            to_z(k, False).start()

    for_heads(8, 16, space_backward)

    @pl.when(zh == core)
    def _():
        total = h3[...].astype(F32)
        for k in range(1, 4):
            to_z(k, True).wait_recv()
            total = total + r4[k - 1].astype(F32)
        for k in range(4):
            to_z(k, False).wait_recv()
            total = total + r4[3 + k].astype(F32)
        h4[...] = total.astype(BF)
        for k in range(1, 4):
            to_all(k, 0).start()
        for k in range(4):
            to_all(k, 1).start()
        r5[x] = h4[...]
        for k in range(1, 4):
            from_all(plus(x, k, 4)).wait_recv()
        for k in range(1, 4):
            to_z(k, True).wait_send()
            to_all(k, 0).wait_send()
        for k in range(4):
            to_all(k, 1).wait_send()

    @pl.when(zh != core)
    def _():
        for k in range(4):
            from_all(plus(x, k, 4)).wait_recv()
        for k in range(4):
            to_z(k, False).wait_send()

    scale = 1.0 / math.sqrt(81920)
    for c in range(4):
        wide = 256 if c < 3 else 384
        wg[:, pl.ds(256 * c, wide)] = r5[c, :, pl.ds(0, wide)].astype(F32) * scale

    for c in range(3):
        gathered(g_items[c])
    gathered(tg_items)
    for src, dst in ((rgq, gqt), (rgk, gkt), (rgv, gvt)):
        dst[0:16] = src[...]
    unpack_arrays(rtg, [gqt, gkt, gvt])

    drained(qkv_items + tq_items + a_items + o_items + tg_items)
    for c in range(3):
        drained(g_items[c])
    w_drained()
    for j in range(4):
        to_sibling(j).wait_send()
        for k in range(1, 4):
            to_x(j, k).wait_send()
    for k in range(1, 8):
        to_y(k).wait_send()


def shards(q_space, k_space, v_space, q_time, k_time, v_time, weight, target):
    tokens = (q_space, k_space, v_space, q_time, k_time, v_time, target)
    flat = [item.reshape(20, 8, D) for item in tokens]
    vm = pl.BlockSpec(memory_space=pltpu.VMEM)

    def buf(*shape, dtype=BF):
        return pltpu.VMEM(shape, dtype)

    tok = buf(20, 8, D)
    main = buf(16, 8, D)
    third = buf(16, 8, 384)
    scratch = [
        buf(2, 16, 36, D), buf(D, D),
        tok, tok, tok, tok,
        main, third, main, third, third, main,
        tok, tok, tok, tok,
        tok, tok, third, tok, tok,
        tok, tok, tok, main, main, main, main,
        buf(HEADS, TOK, TOK, dtype=F32), buf(HEADS, TOK, TOK, dtype=F32), buf(TOK, TOK, dtype=F32),
        buf(D, D), buf(576, D), buf(576, D), buf(3, 576, 384), buf(8, 72, 384),
        buf(7, 72, 384), buf(72, 384), buf(7, 72, 384), buf(72, 384), buf(4, 72, 384),
        pltpu.SemaphoreType.DMA((N_MSG, 16)), pltpu.SemaphoreType.DMA((N_MSG, 16)),
        pltpu.SemaphoreType.DMA((15,)), pltpu.SemaphoreType.DMA((16,)),
        pltpu.SemaphoreType.DMA((4,)), pltpu.SemaphoreType.DMA((4,)),
        pltpu.SemaphoreType.DMA((40,)), pltpu.SemaphoreType.DMA((40,)),
    ]
    out = jax.ShapeDtypeStruct((20, 8, D), BF)
    results = pl.pallas_call(
        kernel,
        out_shape=[out] * 6 + [jax.ShapeDtypeStruct((72, D), F32)],
        in_specs=[vm] * 8,
        out_specs=[vm] * 7,
        scratch_shapes=scratch,
        compiler_params=pltpu.CompilerParams(
            collective_id=0, has_side_effects=True, vmem_limit_bytes=56 * 1024 * 1024
        ),
        name="step",
    )(*flat[:6], weight, flat[6])
    return tuple(item.reshape(q_space.shape) for item in results[:6]) + (results[6],)


def solution(mesh):
    token = P("dp", "seq", None)
    return jax.shard_map(
        shards,
        mesh=mesh,
        in_specs=(token,) * 6 + (P("dp", None), token),
        out_specs=(token,) * 6 + (P("seq", None),),
        check_vma=False,
    )
```

time: 654 us -> 168 us (0.26)
  waiting for transfers between devices: 496 us -> 0 us
  Pallas kernels: 0 us -> 159 us
  starting transfers between devices: 69.2 us -> 0 us
  local copies, waits for them, and re-layouts: 43.3 us -> 8.12 us
  matrix products: 24 us -> 0 us
  between operations: 14.3 us -> 0.66 us
    psum x1 -> x0, waiting for transfers between devices: 259 us -> none  [shards(): total = lax.psum(share, 'dp').astype(jnp.float32)]
    pallas_call x0 -> x1, Pallas kernels: none -> 159 us  [shards(): pl.pallas_call(kernel, out_shape=[out] * 6 + [jax.ShapeDtypeStruct((72, D...]
    unnamed x4 -> x0, waiting for transfers between devices: 139 us -> none
    all_to_all x9 -> x0, waiting for transfers between devices: 97.5 us -> none  [the longest x1 18.7 us: shards(): lax.all_to_all(blocked(q_time), 'seq', split_axis=1, concat_axis=0, tiled...]
    all_to_all x9 -> x0, starting transfers between devices: 68.9 us -> none  [the longest x1 16.2 us: shards(): lax.all_to_all(blocked(q_time), 'seq', split_axis=1, concat_axis=0, tiled...]
    dot_general x13 -> x0, matrix products: 19.9 us -> none  [the longest x2 4.78 us: attend_backward(): jnp.einsum(query_form + ',' + key_form + '->bhlm', step_grad, values, pre...]
    another operation x14 -> x0, local copies, waits for them, and re-layouts: 18.6 us -> none
    reshape x7 -> x0, local copies, waits for them, and re-layouts: 6.82 us -> none  [the longest x4 4.83 us: blocked(): return array.reshape(1, groups, per_block, width)]
  transfers between devices with their start and end apart: 12 -> 0, of which waited for: 10 -> 0; matrix products, arithmetic and copies ran while one was open for 9% -> 0% of each run, Pallas kernels for 0% -> 0%
where the time goes in v1:
time: 168 us
  Pallas kernels  159 us (95%)
  local copies, waits for them, and re-layouts  8.12 us (5%)
    pallas_call x1, Pallas kernels, shards(): pl.pallas_call(kernel, out_shape=[out] * 6 + [jax.ShapeDtypeStruct((72, D...  159 us
    unnamed x19, local copies, waits for them, and re-layouts  8.12 us

profile of v1, /device:TPU:1, one launch (start us, length us, event | category | flops | bytes accessed | tf_op | source)
XLA Modules:
  0.0 168.1 jit_solution(6602218903891722248)
XLA Ops:
  0.6 159.3 %step.1 = (bf16[20,8,1152]{2,1,0:T(8,128)(2,1)}, bf16[20,8,1152]{2,1,0:T(8,128)(2,1)}, bf16[20,8,1152]{2,1,0:T(8,128)(2,1)}, bf16[20,8,1152]{2,1,0:T(8,128)(2,1)...) custom-call(bf16[20,8,1152]{2,1,0:T(8,128)(2,1)} %bitcast.13, ...), custom_call_target="tpu_custom_call" | custom-call | tf_op jit(solution)/shard_map/step/pallas_call | solution.py:574
  160.0 0.0 copy-start.4
  160.0 1.8 %copy.22 = bf16[1,160,1152]{2,1,0:T(8,128)(2,1)} copy(bf16[1,160,1152]{2,1,0:T(8,128)(2,1)} %bitcast.25) | data formatting | bytes 737280
  161.8 0.0 copy-done.4
  161.8 0.0 copy-start.3
  161.8 0.7 copy.23
  162.5 0.4 copy-done.3
  162.9 0.0 copy-start.2
  162.9 0.7 copy.24
  163.6 0.4 copy-done.2
  164.0 0.0 copy-start.1
  164.0 0.7 copy.25
  164.8 0.4 copy-done.1
  165.1 0.0 copy-start
  165.1 0.7 copy.26
  165.9 0.4 copy-done
  166.3 0.0 copy-start.5
  166.3 0.7 copy.27
  167.0 0.4 copy-done.5
  167.4 0.7 copy.28
Async XLA Ops:
  160.0 1.8 %copy-start.4 = (bf16[20,8,1152]{2,1,0:T(8,128)(2,1)S(1)}, bf16[20,8,1152]{2,1,0:T(8,128)(2,1)}, u32[]{:S(2)}) copy-start(bf16[20,8,1152]{2,1,0:T(8,128)(2,1)} %get-tuple-element.15) | copy-start | bytes 1105924
  161.8 1.1 copy-start.3
  162.9 1.1 copy-start.2
  164.0 1.1 copy-start.1
  165.1 1.1 copy-start
  166.3 1.1 copy-start.5

commit v2 on v1

--- a/solution.py
+++ b/solution.py
@@ -17,8 +17,8 @@
 BF = jnp.bfloat16
 F32 = jnp.float32
 MESH = pl.DeviceIdType.MESH
-MQ, MK, MV, MTQ, MA, MTA, MO, MTO, MG, MTG = 0, 1, 2, 3, 4, 5, 6, 7, 8, 17
-N_MSG = 18
+MQ, MTQ, MA, MTA, MO, MTO, MG, MTG = 0, 9, 10, 11, 12, 15, 16, 25
+N_MSG = 26
 
 
 def dot_nn(a, b):
@@ -33,8 +33,8 @@
     return lax.dot_general(a, b, (((0,), (0,)), ((), ())), preferred_element_type=F32)
 
 
-def window(head):
-    start = jnp.minimum((9 * head) // 16, 7) * 128
+def window(head, last=7):
+    start = jnp.minimum((9 * head) // 16, last) * 128
     lanes = lax.broadcasted_iota(jnp.int32, (1, 256), 1) + start
     inside = jnp.logical_and(lanes >= HEAD_DIM * head, lanes < HEAD_DIM * head + HEAD_DIM)
     return pl.ds(pl.multiple_of(start, 128), 256), inside
@@ -53,8 +53,8 @@
     put(ref, cols, jnp.where(inside, value, get(ref, cols).astype(F32)))
 
 
-def forward_head(head, q_ref, k_ref, v_ref, bias_ref, probs_ref, out_ref):
-    cols, inside = window(head)
+def forward_head(head, q_ref, k_ref, v_ref, bias_ref, probs_ref, out_ref, last=7):
+    cols, inside = window(head, last)
     chosen = inside.astype(F32).astype(BF)
     logits = dot_nt(get(q_ref, cols) * chosen, get(k_ref, cols)) * SCALING
     if bias_ref is not None:
@@ -84,6 +84,8 @@
         return carry
 
     lax.fori_loop(0, (last - first) // 2, pair, 0)
+    if (last - first) % 2:
+        step(last - 1)
 
 
 def iota(shape, axis):
@@ -91,12 +93,12 @@
 
 
 def kernel(
-    qs, ks, vs, qt, kt, vt, w_own, target,
-    gqs, gks, gvs, gqt, gkt, gvt, wg,
-    wb, w, rq, rk, rv, ra, rtq, rta, tq, ta, to, tg, space, over, step_b, step_f,
-    ot, ro, rto, comb, gradp, gq, gk, gv, rgq, rgk, rgv, rtg, probs_s, probs_t, bias,
-    wgp, r1, half, r2, h2, r3, h3, r4, h4, r5,
-    ssem, rsem, wsend, wrecv, csend, crecv, rsend, rrecv,
+    qs_in, ks_in, vs_in, qt_in, kt_in, vt_in, w_in, target_in,
+    gqs, gks, gvs, rgq_out, rgk_out, rgv_out, rtg_out, sums,
+    qs, ks, vs, qt, kt, vt, w_own, target, wb, w, rq, rk, rv, ra, rtq, rta, tq, ta, to, tg, space, over, step_b, step_f,
+    ot, ro, rto, comb, gradp, gradt, gq, gk, gv, rgq, rgk, rgv, rtg, probs_s, probs_t, bias,
+    wgp, r1, half, r2, r2n, h2, n2, r3, r3n, h3, h3n, r4, r4n, h4, h4n, r5, r5n,
+    isem, ssem, rsem, wsend, wrecv, csend, crecv, rsend, rrecv,
 ):
     dp = lax.axis_index("dp")
     s = lax.axis_index("seq")
@@ -113,7 +115,21 @@
     def plus(value, k, n):
         return lax.rem(value + k, n)
 
+    def along_z(k):
+        z_ = lax.rem(zh * 4 + zl + k, 8)
+        return device(x, lax.rem(z_, 4), core, z_ // 4, y)
+
     sibling = device(x, zl, 1 - core, zh, y)
+
+    loads = [
+        pltpu.make_async_copy(src, dst, isem.at[n])
+        for n, (src, dst) in enumerate(
+            ((qt_in, qt), (kt_in, kt), (vt_in, vt), (w_in, w_own), (qs_in, qs), (ks_in, ks),
+             (vs_in, vs), (target_in, target))
+        )
+    ]
+    for load in loads:
+        load.start()
 
     barrier = pltpu.get_barrier_semaphore()
 
@@ -128,7 +144,6 @@
         greet(device(plus(x, k, 4), zl, core, zh, y))
         greet(device(plus(x, k, 4), zl, 1 - core, zh, y))
     greet(sibling)
-    pl.semaphore_wait(barrier, 28)
 
     def to_peer(msg, src, dst, peer, cols=None):
         a, b = src.at[peer], dst.at[s]
@@ -148,19 +163,42 @@
             device_id=(dp, peer), device_id_type=MESH,
         )
 
-    def scatter(items):
-        def one(k, carry):
-            peer = plus(s, k, 16)
-            for msg, src, dst, cols in items:
-                to_peer(msg, src, dst, peer, cols).start()
-            return carry
-
-        lax.fori_loop(1, 16, one, 0)
+    def turn(n):
+        return lax.rem((lax.rem(n, 2) * (n + 1) + (1 - lax.rem(n, 2)) * (16 - n)) // 2, 8)
+
+    def send_to(items, peer):
+        for msg, src, dst, cols in items:
+            to_peer(msg, src, dst, peer, cols).start()
+
+    def send_near(items, n):
+        send_to(items, zh * 8 + plus(y, turn(n), 8))
+
+    def send_far(items, n):
+        send_to(items, (1 - zh) * 8 + plus(y, turn(n), 8))
+
+    def keep_own(items):
         for msg, src, dst, cols in items:
             if cols is None:
                 dst[s] = src[s]
             else:
                 dst[s, :, cols] = src[s, :, cols]
+
+    def scatter_near(items):
+        lax.fori_loop(1, 8, lambda n, carry: (send_near(items, n), carry)[1], 0)
+
+    def scatter_far(items):
+        lax.fori_loop(0, 8, lambda n, carry: (send_far(items, n), carry)[1], 0)
+        keep_own(items)
+
+    def scatter(items):
+        def one(n, carry):
+            send_far(items, n)
+            send_near(items, n)
+            return carry
+
+        send_far(items, 0)
+        lax.fori_loop(1, 8, one, 0)
+        keep_own(items)
 
     def gathered(items):
         def one(k, carry):
@@ -180,11 +218,19 @@
 
         lax.fori_loop(1, 16, one, 0)
 
-    qkv_items = [(MQ, qt, rq, None), (MK, kt, rk, None), (MV, vt, rv, None)]
+    thirds = [pl.ds(384 * c, 384) for c in range(3)]
+    qkv_items = [
+        [
+            (MQ + 3 * c, qt, rq, thirds[c]),
+            (MQ + 3 * c + 1, kt, rk, thirds[c]),
+            (MQ + 3 * c + 2, vt, rv, thirds[c]),
+        ]
+        for c in range(3)
+    ]
     tq_items = [(MTQ, tq, rtq, None)]
     a_items = [(MA, over, ra, None), (MTA, ta, rta, None)]
-    o_items = [(MO, ot, ro, None), (MTO, to, rto, None)]
-    thirds = [pl.ds(384 * c, 384) for c in range(3)]
+    o_items = [[(MO + c, ot, ro, thirds[c])] for c in range(3)]
+    to_items = [(MTO, to, rto, None)]
     g_items = [
         [
             (MG + 3 * c, gq, rgq, thirds[c]),
@@ -202,8 +248,8 @@
         )
 
     def w_start():
-        for k in range(1, 4):
-            w_copy(w_own, chip, k - 1, device(x, plus(zl, k, 4), core, zh, y)).start()
+        for n, k in enumerate((1, 7, 2 + 4 * core)):
+            w_copy(w_own, chip, n, along_z(k)).start()
         for k in range(1, 4):
             w_copy(w_own, chip, 2 + k, device(plus(x, k, 4), zl, core, zh, y)).start()
         wb[core, chip] = w_own[...]
@@ -305,22 +351,30 @@
 
         lax.fori_loop(0, 3, one, 0)
 
-    w_start()
-    scatter(qkv_items)
-    pack_arrays([qt, kt, vt], tq)
-    scatter(tq_items)
-
     i, m = iota((TOK, TOK), 0), iota((TOK, TOK), 1)
     patch_i = jnp.where(i < MAIN, lax.rem(i, 8), 8 + lax.rem(i, 2))
     patch_m = jnp.where(m < MAIN, lax.rem(m, 8), 8 + lax.rem(m, 2))
     bias[...] = jnp.where(patch_i == patch_m, 0.0, -1e30)
+    for load in loads[:4]:
+        load.wait()
+    pack_arrays([qt, kt, vt], tq)
+    pl.semaphore_wait(barrier, 28)
+    w_start()
+    scatter_near(tq_items)
+    for c in range(3):
+        scatter_near(qkv_items[c])
+    for load in loads[4:]:
+        load.wait()
 
     def space_forward(h):
         forward_head(h, qs, ks, vs, None, probs_s, space)
 
-    for_heads(0, 6, space_forward)
+    for_heads(0, 8, space_forward)
     w_forward()
-    for_heads(6, 16, space_forward)
+    scatter_far(tq_items)
+    for c in range(3):
+        scatter_far(qkv_items[c])
+    for_heads(8, 16, space_forward)
     w_share()
     w_finish()
 
@@ -335,110 +389,161 @@
 
     in_thirds(back_space)
     pack_thirds(over, ta)
-    scatter(a_items)
-
-    gathered(qkv_items)
+
     gathered(tq_items)
     unpack_arrays(rtq, [rq, rk, rv])
-    for_heads(0, 16, lambda h: forward_head(h, rq, rk, rv, bias, probs_t, ot))
+
+    def time_forward(last):
+        return lambda h: forward_head(h, rq, rk, rv, bias, probs_t, ot, last)
+
+    gathered(qkv_items[0])
+    for_heads(0, 5, time_forward(1))
+    gathered(qkv_items[1])
+    for_heads(5, 10, time_forward(4))
+    scatter(o_items[0])
+    gathered(qkv_items[2])
+    for_heads(10, 12, time_forward(7))
+    scatter(o_items[1])
+    for_heads(12, 16, time_forward(7))
     pack_thirds(ot, to)
-    scatter(o_items)
+    scatter(o_items[2] + to_items)
+    scatter(a_items)
 
     def project_time(cols):
-        put(gradp, cols, dot_nn(get(ot, every), w[:, cols]))
+        put(gradt, cols, dot_nn(get(ot, every), w[:, cols]))
+
+    def back_time(cols):
+        share = dot_nt(get(gradt, every), w[cols, :])
+        put(step_b, cols, share + get(ra, cols).astype(F32))
+
+    def time_backward(h):
+        backward_head(h, rq, rk, rv, probs_t, step_b, gq, gk, gv)
+
+    def send_grads(c):
+        scatter(g_items[c])
+
+    gathered(to_items)
+    for c in range(3):
+        gathered(o_items[c])
+    unpack_thirds(rto, ro)
+    comb[...] = (space[...].astype(F32) + ro[...].astype(F32)).astype(BF)
+
+    def project_all(cols):
+        product = dot_nn(get(comb, every), w[:, cols])
+        put(gradp, cols, product - get(target, cols).astype(F32))
+
+    in_thirds(project_all)
+
+    def to_sibling(j):
+        rows = pl.ds(pl.multiple_of(576 * (1 - core) + 144 * j, 16), 144)
+        return pltpu.make_async_remote_copy(
+            src_ref=wgp.at[rows], dst_ref=r1.at[pl.ds(144 * j, 144)],
+            send_sem=rsend.at[j], recv_sem=rrecv.at[j], device_id=sibling, device_id_type=MESH,
+        )
+
+    def x_window(x_):
+        return pl.ds(pl.multiple_of(256 * x_, 128), 256)
+
+    ninth = pl.ds(1024, 128)
+
+    def to_x(j, k):
+        x_ = plus(x, k, 4)
+        rows = pl.ds(144 * j, 144)
+        return pltpu.make_async_remote_copy(
+            src_ref=half.at[rows, x_window(x_)], dst_ref=r2.at[k - 1, rows],
+            send_sem=rsend.at[4 + 3 * j + k - 1], recv_sem=rrecv.at[4 + 3 * j + k - 1],
+            device_id=device(x_, zl, core, zh, y), device_id_type=MESH,
+        )
+
+    def to_x_ninth(k):
+        x_ = plus(x, k, 4)
+        return pltpu.make_async_remote_copy(
+            src_ref=half.at[pl.ds(pl.multiple_of(144 * x_, 16), 144), ninth], dst_ref=r2n.at[k - 1],
+            send_sem=rsend.at[39 + k], recv_sem=rrecv.at[39 + k],
+            device_id=device(x_, zl, core, zh, y), device_id_type=MESH,
+        )
+
+    def to_y(k):
+        y_ = plus(y, k, 8)
+        return pltpu.make_async_remote_copy(
+            src_ref=h2.at[y_], dst_ref=r3.at[k - 1],
+            send_sem=rsend.at[15 + k], recv_sem=rrecv.at[15 + k],
+            device_id=device(x, zl, core, zh, y_), device_id_type=MESH,
+        )
+
+    def to_y_ninth(n):
+        y_ = 2 * x + n
+        slot = plus(y, 15 - y_, 8)
+        return pltpu.make_async_remote_copy(
+            src_ref=n2.at[n], dst_ref=r3n.at[slot], send_sem=rsend.at[43 + n],
+            recv_sem=rrecv.at[45 + slot], device_id=device(x, zl, core, zh, y_), device_id_type=MESH,
+        )
+
+    def from_y_ninth(slot):
+        return pltpu.make_async_remote_copy(
+            src_ref=n2.at[0], dst_ref=r3n.at[slot], send_sem=rsend.at[43],
+            recv_sem=rrecv.at[45 + slot], device_id=sibling, device_id_type=MESH,
+        )
+
+    def to_z(k, same, ninth_=False):
+        zh_ = zh if same else 1 - zh
+        slot = k - 1 if same else 3 + k
+        src, dst, sem = (h3n, r4n, 52) if ninth_ else (h3, r4, 23)
+        return pltpu.make_async_remote_copy(
+            src_ref=src, dst_ref=dst.at[slot], send_sem=rsend.at[sem + slot],
+            recv_sem=rrecv.at[sem + slot], device_id=device(x, plus(zl, k, 4), core, zh_, y),
+            device_id_type=MESH,
+        )
+
+    def final_peer(k, flip):
+        return device(plus(x, k, 4), zl, core if flip == 0 else 1 - core, zh, y)
+
+    def to_all(k, flip):
+        slot = k - 1 if flip == 0 else 3 + k
+        return pltpu.make_async_remote_copy(
+            src_ref=h4, dst_ref=r5.at[x], send_sem=rsend.at[31 + slot], recv_sem=rrecv.at[31 + x],
+            device_id=final_peer(k, flip), device_id_type=MESH,
+        )
+
+    def to_all_ninth(k, flip):
+        slot = k - 1 if flip == 0 else 3 + k
+        return pltpu.make_async_remote_copy(
+            src_ref=h4n, dst_ref=r5n, send_sem=rsend.at[59 + slot], recv_sem=rrecv.at[59],
+            device_id=final_peer(k, flip), device_id_type=MESH,
+        )
+
+    def from_all(x_):
+        return pltpu.make_async_remote_copy(
+            src_ref=h4, dst_ref=r5.at[x_], send_sem=rsend.at[31], recv_sem=rrecv.at[31 + x_],
+            device_id=sibling, device_id_type=MESH,
+        )
+
+    everyone = [(k, 0) for k in range(1, 4)] + [(k, 1) for k in range(4)]
+    around_z = [(k, True) for k in range(1, 4)] + [(k, False) for k in range(4)]
+    here = zh == core
+    owner = y // 2 == x
+
+    def terms(i, carry):
+        j = core * i + (1 - core) * (8 - i)
+        rows = pl.ds(pl.multiple_of(128 * j, 128), 128)
+        wgp[rows, :] = dot_tn(get(comb, rows), get(gradp, every)).astype(BF)
+        return carry
+
+    def back_all(cols):
+        put(step_f, cols, dot_nt(get(gradp, every), w[cols, :]))
+
+    lax.fori_loop(0, 5, terms, 0)
+    for j in range(4):
+        to_sibling(j).start()
+    lax.fori_loop(5, 9, terms, 0)
+    in_thirds(back_all)
 
     in_thirds(project_time)
     gathered(a_items)
     unpack_thirds(rta, ra)
-
-    def back_time(cols):
-        share = dot_nt(get(gradp, every), w[cols, :])
-        put(step_b, cols, share + get(ra, cols).astype(F32))
-
     in_thirds(back_time)
-
-    def time_backward(h):
-        backward_head(h, rq, rk, rv, probs_t, step_b, gq, gk, gv)
-
-    def send_grads(c):
-        scatter(g_items[c])
-
     for_heads(0, 6, time_backward)
     send_grads(0)
-
-    gathered(o_items)
-    unpack_thirds(rto, ro)
-    comb[...] = (space[...].astype(F32) + ro[...].astype(F32)).astype(BF)
-
-    def project_all(cols):
-        product = dot_nn(get(comb, every), w[:, cols])
-        put(gradp, cols, product - get(target, cols).astype(F32))
-
-    in_thirds(project_all)
-
-    def to_sibling(j):
-        rows = pl.ds(pl.multiple_of(576 * (1 - core) + 144 * j, 16), 144)
-        return pltpu.make_async_remote_copy(
-            src_ref=wgp.at[rows], dst_ref=r1.at[pl.ds(144 * j, 144)],
-            send_sem=rsend.at[j], recv_sem=rrecv.at[j], device_id=sibling, device_id_type=MESH,
-        )
-
-    def x_window(x_):
-        return pl.ds(pl.multiple_of(256 * x_, 128), 384)
-
-    def to_x(j, k):
-        x_ = plus(x, k, 4)
-        rows = pl.ds(144 * j, 144)
-        return pltpu.make_async_remote_copy(
-            src_ref=half.at[rows, x_window(x_)], dst_ref=r2.at[k - 1, rows],
-            send_sem=rsend.at[4 + 3 * j + k - 1], recv_sem=rrecv.at[4 + 3 * j + k - 1],
-            device_id=device(x_, zl, core, zh, y), device_id_type=MESH,
-        )
-
-    def to_y(k):
-        y_ = plus(y, k, 8)
-        return pltpu.make_async_remote_copy(
-            src_ref=h2.at[y_], dst_ref=r3.at[k - 1],
-            send_sem=rsend.at[15 + k], recv_sem=rrecv.at[15 + k],
-            device_id=device(x, zl, core, zh, y_), device_id_type=MESH,
-        )
-
-    def to_z(k, same):
-        zh_ = zh if same else 1 - zh
-        slot = k - 1 if same else 3 + k
-        return pltpu.make_async_remote_copy(
-            src_ref=h3, dst_ref=r4.at[slot], send_sem=rsend.at[23 + slot],
-            recv_sem=rrecv.at[23 + slot], device_id=device(x, plus(zl, k, 4), core, zh_, y),
-            device_id_type=MESH,
-        )
-
-    def to_all(k, flip):
-        slot = k - 1 if flip == 0 else 3 + k
-        return pltpu.make_async_remote_copy(
-            src_ref=h4, dst_ref=r5.at[x], send_sem=rsend.at[31 + slot], recv_sem=rrecv.at[31 + x],
-            device_id=device(plus(x, k, 4), zl, core if flip == 0 else 1 - core, zh, y),
-            device_id_type=MESH,
-        )
-
-    def from_all(x_):
-        return pltpu.make_async_remote_copy(
-            src_ref=h4, dst_ref=r5.at[x_], send_sem=rsend.at[31], recv_sem=rrecv.at[31 + x_],
-            device_id=sibling, device_id_type=MESH,
-        )
-
-    def terms(j, carry):
-        rows = pl.ds(pl.multiple_of(128 * j, 128), 128)
-        wgp[rows, :] = dot_tn(get(comb, rows), get(gradp, every)).astype(BF)
-        return carry
-
-    lax.fori_loop(0, 9, terms, 0)
-    for j in range(4):
-        to_sibling(j).start()
-
-    def back_all(cols):
-        put(step_f, cols, dot_nt(get(gradp, every), w[cols, :]))
-
-    in_thirds(back_all)
 
     for j in range(4):
         to_sibling(j).wait_recv()
@@ -448,12 +553,19 @@
         for k in range(1, 4):
             to_x(j, k).start()
 
+    for k in range(1, 4):
+        to_x_ninth(k).start()
     for_heads(6, 12, time_backward)
     send_grads(1)
     for_heads(12, 16, time_backward)
     send_grads(2)
     pack_arrays([gq, gk, gv], tg)
     scatter(tg_items)
+
+    def space_backward(h):
+        backward_head(h, qs, ks, vs, probs_s, step_f, gqs, gks, gvs)
+
+    for_heads(0, 16, space_backward)
 
     for j in range(4):
         for k in range(1, 4):
@@ -464,13 +576,23 @@
             for k in range(1, 4):
                 total = total + r2[k - 1, rows, :].astype(F32)
             h2[2 * j + i] = total.astype(BF)
-    for k in range(1, 8):
+    for k in (1, 7, 2, 6, 3, 5, 4):
         to_y(k).start()
-
-    def space_backward(h):
-        backward_head(h, qs, ks, vs, probs_s, step_f, gqs, gks, gvs)
-
-    for_heads(0, 8, space_backward)
+    total = half[pl.ds(pl.multiple_of(144 * x, 16), 144), ninth].astype(F32)
+    for k in range(1, 4):
+        to_x_ninth(k).wait_recv()
+        total = total + r2n[k - 1].astype(F32)
+    n2[...] = total.astype(BF).reshape(2, 72, 128)
+    for n in range(2):
+
+        @pl.when(y != 2 * x + n)
+        def _(n=n):
+            to_y_ninth(n).start()
+
+    drained(qkv_items[0] + qkv_items[1] + qkv_items[2])
+    drained(tq_items + a_items + to_items + o_items[0] + o_items[1] + o_items[2])
+    drained(g_items[0] + g_items[1])
+    w_drained()
 
     total = h2[y].astype(F32)
     for k in range(1, 8):
@@ -478,76 +600,130 @@
         total = total + r3[k - 1].astype(F32)
     h3[...] = total.astype(BF)
 
-    @pl.when(zh == core)
+    @pl.when(here)
     def _():
         for k in range(1, 4):
             to_z(k, True).start()
 
-    @pl.when(zh != core)
+    @pl.when(jnp.logical_not(here))
     def _():
         for k in range(4):
             to_z(k, False).start()
 
-    for_heads(8, 16, space_backward)
-
-    @pl.when(zh == core)
+    @pl.when(owner)
+    def _():
+        total = n2[lax.rem(y, 2)].astype(F32)
+        for slot in range(7):
+            from_y_ninth(slot).wait_recv()
+            total = total + r3n[slot].astype(F32)
+        h3n[...] = total.astype(BF)
+
+        @pl.when(here)
+        def _():
+            for k in range(1, 4):
+                to_z(k, True, True).start()
+
+        @pl.when(jnp.logical_not(here))
+        def _():
+            for k in range(4):
+                to_z(k, False, True).start()
+
+    @pl.when(here)
     def _():
         total = h3[...].astype(F32)
-        for k in range(1, 4):
-            to_z(k, True).wait_recv()
-            total = total + r4[k - 1].astype(F32)
-        for k in range(4):
-            to_z(k, False).wait_recv()
-            total = total + r4[3 + k].astype(F32)
+        for n, (k, same) in enumerate(around_z):
+            to_z(k, same).wait_recv()
+            total = total + r4[n].astype(F32)
         h4[...] = total.astype(BF)
-        for k in range(1, 4):
-            to_all(k, 0).start()
-        for k in range(4):
-            to_all(k, 1).start()
+        for k, flip in everyone:
+            to_all(k, flip).start()
         r5[x] = h4[...]
+
+        @pl.when(owner)
+        def _():
+            total = h3n[...].astype(F32)
+            for n, (k, same) in enumerate(around_z):
+                to_z(k, same, True).wait_recv()
+                total = total + r4n[n].astype(F32)
+            h4n[...] = total.astype(BF)
+            for k, flip in everyone:
+                to_all_ninth(k, flip).start()
+            r5n[...] = h4n[...]
+
+        @pl.when(jnp.logical_not(owner))
+        def _():
+            to_all_ninth(0, 1).wait_recv()
+
         for k in range(1, 4):
             from_all(plus(x, k, 4)).wait_recv()
         for k in range(1, 4):
             to_z(k, True).wait_send()
-            to_all(k, 0).wait_send()
-        for k in range(4):
-            to_all(k, 1).wait_send()
-
-    @pl.when(zh != core)
+        for k, flip in everyone:
+            to_all(k, flip).wait_send()
+
+        @pl.when(owner)
+        def _():
+            for k in range(1, 4):
+                to_z(k, True, True).wait_send()
+            for k, flip in everyone:
+                to_all_ninth(k, flip).wait_send()
+
+    @pl.when(jnp.logical_not(here))
     def _():
         for k in range(4):
             from_all(plus(x, k, 4)).wait_recv()
+        to_all_ninth(0, 1).wait_recv()
         for k in range(4):
             to_z(k, False).wait_send()
 
-    scale = 1.0 / math.sqrt(81920)
+        @pl.when(owner)
+        def _():
+            for k in range(4):
+                to_z(k, False, True).wait_send()
+
     for c in range(4):
-        wide = 256 if c < 3 else 384
-        wg[:, pl.ds(256 * c, wide)] = r5[c, :, pl.ds(0, wide)].astype(F32) * scale
+        sums[:, pl.ds(256 * c, 256)] = r5[c]
+    sums[:, ninth] = r5n[...]
 
     for c in range(3):
         gathered(g_items[c])
     gathered(tg_items)
-    for src, dst in ((rgq, gqt), (rgk, gkt), (rgv, gvt)):
-        dst[0:16] = src[...]
-    unpack_arrays(rtg, [gqt, gkt, gvt])
-
-    drained(qkv_items + tq_items + a_items + o_items + tg_items)
-    for c in range(3):
-        drained(g_items[c])
-    w_drained()
+    for src, dst in ((rgq, rgq_out), (rgk, rgk_out), (rgv, rgv_out), (rtg, rtg_out)):
+        dst[...] = src[...]
+
+    drained(g_items[2] + tg_items)
     for j in range(4):
         to_sibling(j).wait_send()
         for k in range(1, 4):
             to_x(j, k).wait_send()
+    for k in range(1, 4):
+        to_x_ninth(k).wait_send()
     for k in range(1, 8):
         to_y(k).wait_send()
+    for n in range(2):
+
+        @pl.when(y != 2 * x + n)
+        def _(n=n):
+            to_y_ninth(n).wait_send()
+
+
+def finish(gqs, gks, gvs, rgq, rgk, rgv, rtg, sums, *out):
+    for src, dst in zip((gqs, gks, gvs), out[:3]):
+        dst[...] = src[...]
+    packed = rtg[...].reshape(128, D)
+    for k, (src, dst) in enumerate(zip((rgq, rgk, rgv), out[3:6])):
+        i, m = iota((32, 128), 0), iota((32, 128), 1)
+        chosen = jnp.where(m == 8 * (i // 2) + 2 * k + lax.rem(i, 2), 1.0, 0.0).astype(BF)
+        dst[0:16] = src[...]
+        dst[16:20] = dot_nn(chosen, packed).astype(BF).reshape(4, 8, D)
+    out[6][...] = sums[...].astype(F32) * (1.0 / math.sqrt(81920))
 
 
 def shards(q_space, k_space, v_space, q_time, k_time, v_time, weight, target):
     tokens = (q_space, k_space, v_space, q_time, k_time, v_time, target)
     flat = [item.reshape(20, 8, D) for item in tokens]
     vm = pl.BlockSpec(memory_space=pltpu.VMEM)
+    anywhere = pl.BlockSpec(memory_space=pltpu.HBM)
 
     def buf(*shape, dtype=BF):
         return pltpu.VMEM(shape, dtype)
@@ -556,32 +732,45 @@
     main = buf(16, 8, D)
     third = buf(16, 8, 384)
     scratch = [
+        tok, tok, tok, tok, tok, tok, buf(36, D), tok,
         buf(2, 16, 36, D), buf(D, D),
         tok, tok, tok, tok,
         main, third, main, third, third, main,
         tok, tok, tok, tok,
-        tok, tok, third, tok, tok,
+        tok, tok, third, tok, tok, tok,
         tok, tok, tok, main, main, main, main,
         buf(HEADS, TOK, TOK, dtype=F32), buf(HEADS, TOK, TOK, dtype=F32), buf(TOK, TOK, dtype=F32),
-        buf(D, D), buf(576, D), buf(576, D), buf(3, 576, 384), buf(8, 72, 384),
-        buf(7, 72, 384), buf(72, 384), buf(7, 72, 384), buf(72, 384), buf(4, 72, 384),
+        buf(D, D), buf(576, D), buf(576, D), buf(3, 576, 256), buf(3, 144, 128),
+        buf(8, 72, 256), buf(2, 72, 128), buf(7, 72, 256), buf(7, 72, 128),
+        buf(72, 256), buf(72, 128), buf(7, 72, 256), buf(7, 72, 128),
+        buf(72, 256), buf(72, 128), buf(4, 72, 256), buf(72, 128),
+        pltpu.SemaphoreType.DMA((8,)),
         pltpu.SemaphoreType.DMA((N_MSG, 16)), pltpu.SemaphoreType.DMA((N_MSG, 16)),
         pltpu.SemaphoreType.DMA((15,)), pltpu.SemaphoreType.DMA((16,)),
         pltpu.SemaphoreType.DMA((4,)), pltpu.SemaphoreType.DMA((4,)),
-        pltpu.SemaphoreType.DMA((40,)), pltpu.SemaphoreType.DMA((40,)),
+        pltpu.SemaphoreType.DMA((68,)), pltpu.SemaphoreType.DMA((68,)),
     ]
     out = jax.ShapeDtypeStruct((20, 8, D), BF)
-    results = pl.pallas_call(
+    part = jax.ShapeDtypeStruct((16, 8, D), BF)
+    middle = pl.pallas_call(
         kernel,
-        out_shape=[out] * 6 + [jax.ShapeDtypeStruct((72, D), F32)],
-        in_specs=[vm] * 8,
-        out_specs=[vm] * 7,
+        out_shape=[out] * 3 + [part] * 4 + [jax.ShapeDtypeStruct((72, D), BF)],
+        in_specs=[anywhere] * 8,
+        out_specs=[vm] * 8,
         scratch_shapes=scratch,
         compiler_params=pltpu.CompilerParams(
             collective_id=0, has_side_effects=True, vmem_limit_bytes=56 * 1024 * 1024
         ),
         name="step",
     )(*flat[:6], weight, flat[6])
+    results = pl.pallas_call(
+        finish,
+        out_shape=[out] * 6 + [jax.ShapeDtypeStruct((72, D), F32)],
+        in_specs=[vm] * 8,
+        out_specs=[vm] * 7,
+        compiler_params=pltpu.CompilerParams(vmem_limit_bytes=60 * 1024 * 1024),
+        name="finish",
+    )(*middle)
     return tuple(item.reshape(q_space.shape) for item in results[:6]) + (results[6],)
 
 

time: 168 us -> 147 us (0.88)
  Pallas kernels: 159 us -> 146 us
  local copies, waits for them, and re-layouts: 8.12 us -> 0 us
    pallas_call x1 -> x2, Pallas kernels: 159 us -> 146 us  [the longest x1 143 us: shards(): pl.pallas_call(kernel, out_shape=[out] * 3 + [part] * 4 + [jax.ShapeDtype...]
    unnamed x19 -> x0, local copies, waits for them, and re-layouts: 8.12 us -> none
where the time goes in v2:
time: 147 us
  Pallas kernels  146 us (99%)
    pallas_call x1, Pallas kernels, shards(): pl.pallas_call(kernel, out_shape=[out] * 3 + [part] * 4 + [jax.ShapeDtype...  143 us
    pallas_call x1, Pallas kernels, shards(): pl.pallas_call(finish, out_shape=[out] * 6 + [jax.ShapeDtypeStruct((72, D...  3.27 us

profile of v2, /device:TPU:1, one launch (start us, length us, event | category | flops | bytes accessed | tf_op | source)
XLA Modules:
  0.0 146.5 jit_solution(15294384001224948176)
XLA Ops:
  0.6 142.6 %step.1 = (bf16[20,8,1152]{2,1,0:T(8,128)(2,1)}, bf16[20,8,1152]{2,1,0:T(8,128)(2,1)}, bf16[20,8,1152]{2,1,0:T(8,128)(2,1)}, bf16[16,8,1152]{2,1,0:T(8,128)(2,1)...) custom-call(bf16[20,8,1152]{2,1,0:T(8,128)(2,1)} %bitcast.13, ...), custom_call_target="tpu_custom_call" | custom-call | tf_op jit(solution)/shard_map/step/pallas_call | solution.py:755
  143.2 3.3 %finish.1 = (bf16[20,8,1152]{2,1,0:T(8,128)(2,1)}, bf16[20,8,1152]{2,1,0:T(8,128)(2,1)}, bf16[20,8,1152]{2,1,0:T(8,128)(2,1)}, bf16[20,8,1152]{2,1,0:T(8,128)(2,...) custom-call(bf16[20,8,1152]{2,1,0:T(8,128)(2,1)} %get-tuple-element.22.gqs, ...), custom_call_target="tpu_custom_call" | custom-call | tf_op jit(solution)/shard_map/finish/pallas_call | solution.py:766

commit v3 on v2

--- a/solution.py
+++ b/solution.py
@@ -389,6 +389,7 @@
 
     in_thirds(back_space)
     pack_thirds(over, ta)
+    scatter_near(a_items)
 
     gathered(tq_items)
     unpack_arrays(rtq, [rq, rk, rv])
@@ -399,6 +400,7 @@
     gathered(qkv_items[0])
     for_heads(0, 5, time_forward(1))
     gathered(qkv_items[1])
+    scatter_far(a_items)
     for_heads(5, 10, time_forward(4))
     scatter(o_items[0])
     gathered(qkv_items[2])
@@ -407,10 +409,11 @@
     for_heads(12, 16, time_forward(7))
     pack_thirds(ot, to)
     scatter(o_items[2] + to_items)
-    scatter(a_items)
 
     def project_time(cols):
         put(gradt, cols, dot_nn(get(ot, every), w[:, cols]))
+
+    in_thirds(project_time)
 
     def back_time(cols):
         share = dot_nt(get(gradt, every), w[cols, :])
@@ -421,6 +424,12 @@
 
     def send_grads(c):
         scatter(g_items[c])
+
+    gathered(a_items)
+    unpack_thirds(rta, ra)
+    in_thirds(back_time)
+    for_heads(0, 6, time_backward)
+    send_grads(0)
 
     gathered(to_items)
     for c in range(3):
@@ -536,14 +545,9 @@
     for j in range(4):
         to_sibling(j).start()
     lax.fori_loop(5, 9, terms, 0)
-    in_thirds(back_all)
-
-    in_thirds(project_time)
-    gathered(a_items)
-    unpack_thirds(rta, ra)
-    in_thirds(back_time)
-    for_heads(0, 6, time_backward)
-    send_grads(0)
+
+    for_heads(6, 12, time_backward)
+    send_grads(1)
 
     for j in range(4):
         to_sibling(j).wait_recv()
@@ -555,8 +559,6 @@
 
     for k in range(1, 4):
         to_x_ninth(k).start()
-    for_heads(6, 12, time_backward)
-    send_grads(1)
     for_heads(12, 16, time_backward)
     send_grads(2)
     pack_arrays([gq, gk, gv], tg)
@@ -565,6 +567,7 @@
     def space_backward(h):
         backward_head(h, qs, ks, vs, probs_s, step_f, gqs, gks, gvs)
 
+    in_thirds(back_all)
     for_heads(0, 16, space_backward)
 
     for j in range(4):

time: 147 us -> 142 us (0.966)
  Pallas kernels: 146 us -> 140 us
    pallas_call x1, Pallas kernels: 143 us -> 137 us  [shards(): pl.pallas_call(kernel, out_shape=[out] * 3 + [part] * 4 + [jax.ShapeDtype...]
where the time goes in v3:
time: 142 us; the launch traced here: 141 us
  Pallas kernels  140 us (99%)
    pallas_call x1, Pallas kernels, shards(): pl.pallas_call(kernel, out_shape=[out] * 3 + [part] * 4 + [jax.ShapeDtype...  137 us
    pallas_call x1, Pallas kernels, shards(): pl.pallas_call(finish, out_shape=[out] * 6 + [jax.ShapeDtypeStruct((72, D...  3.27 us

profile of v3, /device:TPU:1, one launch (start us, length us, event | category | flops | bytes accessed | tf_op | source)
XLA Modules:
  0.0 140.7 jit_solution(17298889903551397834)
XLA Ops:
  0.6 136.8 %step.1 = (bf16[20,8,1152]{2,1,0:T(8,128)(2,1)}, bf16[20,8,1152]{2,1,0:T(8,128)(2,1)}, bf16[20,8,1152]{2,1,0:T(8,128)(2,1)}, bf16[16,8,1152]{2,1,0:T(8,128)(2,1)...) custom-call(bf16[20,8,1152]{2,1,0:T(8,128)(2,1)} %bitcast.13, ...), custom_call_target="tpu_custom_call" | custom-call | tf_op jit(solution)/shard_map/step/pallas_call | solution.py:758
  137.4 3.3 %finish.1 = (bf16[20,8,1152]{2,1,0:T(8,128)(2,1)}, bf16[20,8,1152]{2,1,0:T(8,128)(2,1)}, bf16[20,8,1152]{2,1,0:T(8,128)(2,1)}, bf16[20,8,1152]{2,1,0:T(8,128)(2,...) custom-call(bf16[20,8,1152]{2,1,0:T(8,128)(2,1)} %get-tuple-element.22.gqs, ...), custom_call_target="tpu_custom_call" | custom-call | tf_op jit(solution)/shard_map/finish/pallas_call | solution.py:769
